TPU v7x, 32 devices: a whole 2x2x4 slice. The times are simulated.
32 devices in a mesh: dp: 8 (over z, x), tensor: 4 (over y, core).
Axes of the slice: x: 2, y: 2, z: 4, core: 2. Of those that a mesh axis runs over, the one named last changes fastest.
Arguments:
- tokens: bfloat16 [128, 64, 768], P('dp'), may hold values from -6 to 6
- image_tokens: bfloat16 [128, 256, 768], P('dp', None, 'tensor'), may hold values from -6 to 6
- image_counts: int32 [128], P('dp'), may hold values from 64 to 256, as said below
- ln1_gain: float32 [768], replicated, may hold values from 0.25 to 1.75
- ln1_bias: float32 [768], replicated, may hold values from -2 to 2
- self_qkv: bfloat16 [768, 3, 768], P(None, None, 'tensor'), may hold values from -0.21875 to 0.21875
- self_output_weight: bfloat16 [768, 768], P('tensor'), may hold values from -0.625 to 0.625
- self_output_bias: float32 [768], replicated, may hold values from -2 to 2
- ln2_gain: float32 [768], replicated, may hold values from 0.25 to 1.75
- ln2_bias: float32 [768], replicated, may hold values from -2 to 2
- cross_query_weight: bfloat16 [768, 768], P(None, 'tensor'), may hold values from -0.21875 to 0.21875
- cross_kv: bfloat16 [768, 2, 768], P(None, None, 'tensor'), may hold values from -0.21875 to 0.21875
- cross_output_weight: bfloat16 [768, 768], P('tensor'), may hold values from -0.625 to 0.625
- cross_output_bias: float32 [768], replicated, may hold values from -2 to 2
- ln3_gain: float32 [768], replicated, may hold values from 0.25 to 1.75
- ln3_bias: float32 [768], replicated, may hold values from -2 to 2
- mlp_in: bfloat16 [768, 3072], P(None, 'tensor'), may hold values from -0.21875 to 0.21875
- mlp_in_bias: float32 [3072], P('tensor'), may hold values from -3 to 3
- mlp_out: bfloat16 [3072, 768], P('tensor'), may hold values from -0.15625 to 0.15625
- mlp_out_bias: float32 [768], replicated, may hold values from -2 to 2
- grad_out: bfloat16 [128, 64, 768], P('dp'), may hold values from -6 to 6
Outputs:
- output: bfloat16 [128, 64, 768], P('dp')
- grad_tokens: bfloat16 [128, 64, 768], P('dp')
- grad_image: bfloat16 [128, 256, 768], P('dp', None, 'tensor')
- grad_ln1_gain: float32 [768], replicated
- grad_ln1_bias: float32 [768], replicated
- grad_self_qkv: float32 [768, 3, 768], P('dp', None, 'tensor')
- grad_self_out: float32 [768, 768], P('tensor', 'dp')
- grad_self_out_bias: float32 [768], replicated
- grad_ln2_gain: float32 [768], replicated
- grad_ln2_bias: float32 [768], replicated
- grad_cross_q: float32 [768, 768], P('dp', 'tensor')
- grad_cross_kv: float32 [768, 2, 768], P('dp', None, 'tensor')
- grad_cross_out: float32 [768, 768], P('tensor', 'dp')
- grad_cross_out_bias: float32 [768], replicated
- grad_ln3_gain: float32 [768], replicated
- grad_ln3_bias: float32 [768], replicated
- grad_mlp_in: float32 [768, 3072], P('dp', 'tensor')
- grad_mlp_in_bias: float32 [3072], P('tensor')
- grad_mlp_out: float32 [3072, 768], P('tensor', 'dp')
- grad_mlp_out_bias: float32 [768], replicated
Inputs may be any that keep to these rules, and one draw needn't show every extreme that they name: image_counts[c] is the number of leading image tokens that caption c attends to; both bounds are reached in every draw.
All inputs are finite; a program needn't handle non-finite values.
Results may differ from a plain program's by a relative error of at most 0.034.
Values may be sent and summed in bfloat16 or wider, within the bound.
A program may use at most 192 MiB of HBM per device.

v0:
```python
from functools import partial
import jax
import jax.numpy as jnp
from jax import lax
from jax.sharding import PartitionSpec as P

HEAD_SIZE = 64


def norm_parts(values):
    center = values - jnp.mean(values, axis=-1, keepdims=True)
    inv_std = lax.rsqrt(jnp.mean(center * center, axis=-1, keepdims=True) + 1e-05)
    return (center * inv_std, inv_std)


def norm_back(gradient, normed, inv_std, gain_row):
    scaled = gradient * gain_row
    return inv_std * (
        scaled
        - jnp.mean(scaled, axis=-1, keepdims=True)
        - normed * jnp.mean(scaled * normed, axis=-1, keepdims=True)
    )


def branch_total(term_rows):
    return lax.psum(term_rows.astype(jnp.bfloat16), "tensor").astype(jnp.float32)


def input_total(term_rows):
    return lax.psum(term_rows.astype(jnp.bfloat16), "tensor").astype(jnp.float32)


def attend_forward(queries, key_rows, value_rows, allowed, scaling):
    scores = (
        jnp.einsum("clhe,cmhe->chlm", queries, key_rows, preferred_element_type=jnp.float32)
        * scaling
    )
    scores = jnp.where(allowed[:, None], scores, -1000000000.0)
    highest = jnp.max(scores, axis=-1, keepdims=True)
    exponent = jnp.exp(scores - highest)
    chances = exponent / jnp.sum(exponent, axis=-1, keepdims=True)
    mixture = jnp.einsum(
        "chlm,cmhe->clhe",
        chances.astype(jnp.bfloat16),
        value_rows,
        preferred_element_type=jnp.float32,
    )
    return (mixture.astype(jnp.bfloat16), chances)


def attend_back(grad_mixture, queries, key_rows, value_rows, chances, scaling):
    grad_chances = jnp.einsum(
        "clhe,cmhe->chlm", grad_mixture, value_rows, preferred_element_type=jnp.float32
    )
    grad_values = jnp.einsum(
        "chlm,clhe->cmhe",
        chances.astype(jnp.bfloat16),
        grad_mixture,
        preferred_element_type=jnp.float32,
    )
    inner_sum = jnp.sum(grad_chances * chances, axis=-1, keepdims=True)
    grad_scores = (chances * (grad_chances - inner_sum)).astype(jnp.bfloat16)
    grad_queries = (
        jnp.einsum("chlm,cmhe->clhe", grad_scores, key_rows, preferred_element_type=jnp.float32)
        * scaling
    )
    grad_keys = (
        jnp.einsum("chlm,clhe->cmhe", grad_scores, queries, preferred_element_type=jnp.float32)
        * scaling
    )
    return (
        grad_queries.astype(jnp.bfloat16),
        grad_keys.astype(jnp.bfloat16),
        grad_values.astype(jnp.bfloat16),
    )


def local(
    tokens,
    image_tokens,
    image_counts,
    ln1_gain,
    ln1_bias,
    self_qkv,
    self_output_weight,
    self_output_bias,
    ln2_gain,
    ln2_bias,
    cross_query_weight,
    cross_kv,
    cross_output_weight,
    cross_output_bias,
    ln3_gain,
    ln3_bias,
    mlp_in,
    mlp_in_bias,
    mlp_out,
    mlp_out_bias,
    grad_out,
):
    captions, length, model_width = tokens.shape
    row_count = captions * length
    local_width = self_output_weight.shape[0]
    local_heads = local_width // HEAD_SIZE
    scaling = HEAD_SIZE ** (-0.5)
    residual = tokens.astype(jnp.float32).reshape(row_count, model_width)
    normed_one, inv_one = norm_parts(residual)
    in_one = (normed_one * ln1_gain + ln1_bias).astype(jnp.bfloat16)
    qkv_rows = jnp.einsum(
        "rd,dtk->rtk", in_one, self_qkv, preferred_element_type=jnp.float32
    ).astype(jnp.bfloat16)
    qkv_view = qkv_rows.reshape(captions, length, 3, local_heads, HEAD_SIZE)
    queries_one, keys_one, values_one = (qkv_view[:, :, 0], qkv_view[:, :, 1], qkv_view[:, :, 2])
    positions = jnp.arange(length)
    causal = jnp.broadcast_to(positions[:, None] >= positions[None, :], (captions, length, length))
    mixture_one, chances_one = attend_forward(queries_one, keys_one, values_one, causal, scaling)
    mixture_one = mixture_one.reshape(row_count, local_width)
    after_first_residual = (
        residual
        + branch_total(jnp.dot(mixture_one, self_output_weight, preferred_element_type=jnp.float32))
        + self_output_bias
    )
    second_normalized, inv_two = norm_parts(after_first_residual)
    in_two = (second_normalized * ln2_gain + ln2_bias).astype(jnp.bfloat16)
    second_query_rows = (
        jnp.dot(in_two, cross_query_weight, preferred_element_type=jnp.float32)
        .astype(jnp.bfloat16)
        .reshape(captions, length, local_heads, HEAD_SIZE)
    )
    image_full = lax.all_gather(image_tokens, "tensor", axis=2, tiled=True)
    image_count = image_full.shape[1]
    kv_rows = jnp.einsum(
        "cid,dtk->citk", image_full, cross_kv, preferred_element_type=jnp.float32
    ).astype(jnp.bfloat16)
    kv_view = kv_rows.reshape(captions, image_count, 2, local_heads, HEAD_SIZE)
    keys_two, values_two = (kv_view[:, :, 0], kv_view[:, :, 1])
    valid_keys = jnp.arange(image_count)[None, :] < image_counts[:, None]
    cross_mask = jnp.broadcast_to(valid_keys[:, None, :], (captions, length, image_count))
    mixture_two, chances_two = attend_forward(
        second_query_rows, keys_two, values_two, cross_mask, scaling
    )
    mixture_two = mixture_two.reshape(row_count, local_width)
    after_second_residual = (
        after_first_residual
        + branch_total(
            jnp.dot(mixture_two, cross_output_weight, preferred_element_type=jnp.float32)
        )
        + cross_output_bias
    )
    normed_three, inv_three = norm_parts(after_second_residual)
    in_three = (normed_three * ln3_gain + ln3_bias).astype(jnp.bfloat16)
    pre_act = jnp.dot(in_three, mlp_in, preferred_element_type=jnp.float32) + mlp_in_bias
    activated, gelu_pull = jax.vjp(partial(jax.nn.gelu, approximate=False), pre_act)
    act_low = activated.astype(jnp.bfloat16)
    result = (
        after_second_residual
        + branch_total(jnp.dot(act_low, mlp_out, preferred_element_type=jnp.float32))
        + mlp_out_bias
    )
    output = result.astype(jnp.bfloat16).reshape(tokens.shape)
    grad_rows = grad_out.astype(jnp.float32).reshape(row_count, model_width)
    grad_low = grad_rows.astype(jnp.bfloat16)
    grad_mlp_out_local = jnp.einsum(
        "rf,rd->fd", act_low, grad_low, preferred_element_type=jnp.float32
    )
    grad_hidden = jnp.einsum("rd,fd->rf", grad_low, mlp_out, preferred_element_type=jnp.float32)
    (grad_pre,) = gelu_pull(grad_hidden)
    grad_pre_low = grad_pre.astype(jnp.bfloat16)
    grad_mlp_in_bias = jnp.sum(grad_pre_low, axis=0, dtype=jnp.float32)
    grad_mlp_in_local = jnp.einsum(
        "rd,rf->df", in_three, grad_pre_low, preferred_element_type=jnp.float32
    )
    grad_in_three = input_total(
        jnp.einsum("rf,df->rd", grad_pre_low, mlp_in, preferred_element_type=jnp.float32)
    )
    grad_gain_three = jnp.sum(grad_in_three * normed_three, axis=0)
    grad_bias_three = jnp.sum(grad_in_three, axis=0)
    grad_two = grad_rows + norm_back(grad_in_three, normed_three, inv_three, ln3_gain)
    grad_two_low = grad_two.astype(jnp.bfloat16)
    grad_cross_bias = jnp.sum(grad_two, axis=0)
    grad_cross_out_local = jnp.einsum(
        "rk,rd->kd", mixture_two, grad_two_low, preferred_element_type=jnp.float32
    )
    grad_mix_two = jnp.einsum(
        "rd,kd->rk", grad_two_low, cross_output_weight, preferred_element_type=jnp.float32
    ).astype(jnp.bfloat16)
    grad_mix_two = grad_mix_two.reshape(captions, length, local_heads, HEAD_SIZE)
    grad_query_two, grad_keys_two, grad_values_two = attend_back(
        grad_mix_two, second_query_rows, keys_two, values_two, chances_two, scaling
    )
    grad_kv = jnp.stack([grad_keys_two, grad_values_two], axis=2).reshape(
        captions, image_count, 2, local_width
    )
    grad_cross_kv_local = jnp.einsum(
        "cid,citk->dtk", image_full, grad_kv, preferred_element_type=jnp.float32
    )
    image_terms = jnp.einsum("citk,dtk->cid", grad_kv, cross_kv, preferred_element_type=jnp.float32)
    grad_image = lax.psum_scatter(
        image_terms.astype(jnp.bfloat16), "tensor", scatter_dimension=2, tiled=True
    )
    query_rows_two = grad_query_two.reshape(row_count, local_width)
    grad_cross_q_local = jnp.einsum(
        "rd,rk->dk", in_two, query_rows_two, preferred_element_type=jnp.float32
    )
    grad_in_two = input_total(
        jnp.einsum(
            "rk,dk->rd", query_rows_two, cross_query_weight, preferred_element_type=jnp.float32
        )
    )
    grad_gain_two = jnp.sum(grad_in_two * second_normalized, axis=0)
    grad_bias_two = jnp.sum(grad_in_two, axis=0)
    grad_one = grad_two + norm_back(grad_in_two, second_normalized, inv_two, ln2_gain)
    grad_one_low = grad_one.astype(jnp.bfloat16)
    grad_self_bias = jnp.sum(grad_one, axis=0)
    grad_self_out_local = jnp.einsum(
        "rk,rd->kd", mixture_one, grad_one_low, preferred_element_type=jnp.float32
    )
    grad_mix_one = jnp.einsum(
        "rd,kd->rk", grad_one_low, self_output_weight, preferred_element_type=jnp.float32
    ).astype(jnp.bfloat16)
    grad_mix_one = grad_mix_one.reshape(captions, length, local_heads, HEAD_SIZE)
    grad_query_one, grad_keys_one, grad_values_one = attend_back(
        grad_mix_one, queries_one, keys_one, values_one, chances_one, scaling
    )
    grad_qkv = jnp.stack([grad_query_one, grad_keys_one, grad_values_one], axis=2).reshape(
        row_count, 3, local_width
    )
    grad_self_qkv_local = jnp.einsum(
        "rd,rtk->dtk", in_one, grad_qkv, preferred_element_type=jnp.float32
    )
    grad_in_one = input_total(
        jnp.einsum("rtk,dtk->rd", grad_qkv, self_qkv, preferred_element_type=jnp.float32)
    )
    grad_gain_one = jnp.sum(grad_in_one * normed_one, axis=0)
    grad_bias_one = jnp.sum(grad_in_one, axis=0)
    grad_tokens = (
        (grad_one + norm_back(grad_in_one, normed_one, inv_one, ln1_gain))
        .astype(jnp.bfloat16)
        .reshape(tokens.shape)
    )
    grad_out_bias = jnp.sum(grad_rows, axis=0)
    (
        grad_self_qkv,
        grad_self_out,
        grad_cross_q,
        grad_cross_kv,
        grad_cross_out,
        grad_mlp_in,
        grad_mlp_out,
    ) = (
        lax.psum_scatter(grad_self_qkv_local, "dp", scatter_dimension=0, tiled=True),
        lax.psum_scatter(grad_self_out_local, "dp", scatter_dimension=1, tiled=True),
        lax.psum_scatter(grad_cross_q_local, "dp", scatter_dimension=0, tiled=True),
        lax.psum_scatter(grad_cross_kv_local, "dp", scatter_dimension=0, tiled=True),
        lax.psum_scatter(grad_cross_out_local, "dp", scatter_dimension=1, tiled=True),
        lax.psum_scatter(grad_mlp_in_local, "dp", scatter_dimension=0, tiled=True),
        lax.psum_scatter(grad_mlp_out_local, "dp", scatter_dimension=1, tiled=True),
    )
    (
        grad_gain_one,
        grad_bias_one,
        grad_self_bias,
        grad_gain_two,
        grad_bias_two,
        grad_cross_bias,
        grad_gain_three,
        grad_bias_three,
        grad_mlp_in_bias,
        grad_out_bias,
    ) = lax.psum(
        (
            grad_gain_one,
            grad_bias_one,
            grad_self_bias,
            grad_gain_two,
            grad_bias_two,
            grad_cross_bias,
            grad_gain_three,
            grad_bias_three,
            grad_mlp_in_bias,
            grad_out_bias,
        ),
        "dp",
    )
    return (
        output,
        grad_tokens,
        grad_image,
        grad_gain_one,
        grad_bias_one,
        grad_self_qkv,
        grad_self_out,
        grad_self_bias,
        grad_gain_two,
        grad_bias_two,
        grad_cross_q,
        grad_cross_kv,
        grad_cross_out,
        grad_cross_bias,
        grad_gain_three,
        grad_bias_three,
        grad_mlp_in,
        grad_mlp_in_bias,
        grad_mlp_out,
        grad_out_bias,
    )


def solution(mesh):
    return jax.shard_map(
        local,
        mesh=mesh,
        in_specs=(
            P("dp", None, None),
            P("dp", None, "tensor"),
            P("dp"),
            P(),
            P(),
            P(None, None, "tensor"),
            P("tensor", None),
            P(),
            P(),
            P(),
            P(None, "tensor"),
            P(None, None, "tensor"),
            P("tensor", None),
            P(),
            P(),
            P(),
            P(None, "tensor"),
            P("tensor"),
            P("tensor", None),
            P(),
            P("dp", None, None),
        ),
        out_specs=(
            P("dp", None, None),
            P("dp", None, None),
            P("dp", None, "tensor"),
            P(),
            P(),
            P("dp", None, "tensor"),
            P("tensor", "dp"),
            P(),
            P(),
            P(),
            P("dp", "tensor"),
            P("dp", None, "tensor"),
            P("tensor", "dp"),
            P(),
            P(),
            P(),
            P("dp", "tensor"),
            P("tensor"),
            P("tensor", "dp"),
            P(),
        ),
        check_vma=False,
    )
```

profile of v0, /device:TPU:0, one launch (start us, length us, event | category | flops | bytes accessed | tf_op | source)
XLA Modules:
  0.0 956.3 jit_solution(9521117675636398474)
XLA Ops:
  14.8 4.2 reshape.186
  19.0 3.1 fusion.96
  24.0 2.7 copy.154
  29.5 2.1 fusion.97
  31.6 3.6 fusion.59
  35.3 2.5 copy.103
  37.8 2.4 reshape.187
  40.2 2.8 convolution_convert_fusion.5
  44.7 44.1 %all-reduce.8.cloned.1.call-done = bf16[1024,768]{1,0:T(8,128)(2,1)} async-done(((bf16[1024,768]{1,0:T(8,128)(2,1)}), bf16[1024,768]{1,0:T(8,128)(2,1)}) %all-reduce.8.cloned.1.call-update) | async-done | bytes 1572880 | tf_op jit(solution)/shard_map/psum | solution.py:26
  95.4 2.4 reshape.189
  97.8 39.0 %all-gather.2.cloned.1.call-done = bf16[16,256,768]{1,2,0:T(8,128)(2,1)} async-done(((bf16[16,256,192]{1,2,0:T(8,128)(2,1)}), bf16[16,256,768]{1,2,0:T(8,128)(2,1)}) %all-gather.2.cloned.1.call-update) | async-done | bytes 6291472 | tf_op jit(solution)/shard_map/all_gather | solution.py:130
  136.8 5.6 fusion.46
  143.1 3.2 fusion.98
  149.4 2.4 reshape.190
  151.8 2.9 convolution_convert_fusion.4
  155.0 2.7 bitcast_convert_fusion.2
  157.7 40.0 %all-reduce.10.cloned.1.call-done = bf16[1024,768]{1,0:T(8,128)(2,1)} async-done(((bf16[1024,768]{1,0:T(8,128)(2,1)}), bf16[1024,768]{1,0:T(8,128)(2,1)}) %all-reduce.10.cloned.1.call-update) | async-done | bytes 1572880 | tf_op jit(solution)/shard_map/psum | solution.py:26
  197.7 2.8 fusion.95
  204.9 10.3 %convert_reduce_fusion.5 = (f32[768]{0:T(1024)}, bf16[1024,768]{1,0:T(8,128)(2,1)S(1)}, f32[1024,768]{1,0:T(8,128)}) fusion(f32[1024,768]{1,0:T(8,128)S(1)} %fusion.100, f32[768]{0:T(1024)S(1)} %copy-done.59, bf16[1024,768]{1,0:T(8,128)(2,1)S(1)} %copy-done.29, bf16[768,768]{1,0:T(8,128)(2,1)S(1)} %copy-done), kind=kOutput, calls=%fused_computation.59 | convolution fusion | flops 1266941184 | bytes 10622976 | tf_op jit(solution)/shard_map/rd,fd->rf/dot_general | solution.py:166
  216.3 2.6 convolution_convert_fusion.2
  219.3 4.4 multiply_convert_fusion.2
  223.7 38.3 %all-reduce.12.cloned.1.call-done = bf16[1024,768]{1,0:T(8,128)(2,1)} async-done(((bf16[1024,768]{1,0:T(8,128)(2,1)}), bf16[1024,768]{1,0:T(8,128)(2,1)}) %all-reduce.12.cloned.1.call-update) | async-done | bytes 1572880 | tf_op jit(solution)/shard_map/psum | solution.py:30
  262.0 4.4 fusion.29
  266.4 3.2 fusion.91
  272.7 2.4 reshape.193
  275.1 4.0 multiply_reduce_fusion
  282.8 2.6 copy.110
  285.4 2.4 reshape.194
  287.8 2.9 convolution_convert_fusion.1
  290.8 4.1 convolution_convert_fusion.3
  299.2 11.6 %reduce-scatter.25.cloned.1.call-start = ((), (), s32[]{:S(2)}) async-start(), calls=%async_computation.18 | async-start | bytes 884736
  310.8 23.0 %all-reduce.14.cloned.1.call-done = bf16[1024,768]{1,0:T(8,128)(2,1)} async-done(((bf16[1024,768]{1,0:T(8,128)(2,1)}), bf16[1024,768]{1,0:T(8,128)(2,1)}) %all-reduce.14.cloned.1.call-update) | async-done | bytes 1572880 | tf_op jit(solution)/shard_map/psum | solution.py:30
  333.8 4.2 fusion.30
  338.0 3.5 fusion.93
  344.9 2.9 convolution_convert_fusion
  347.7 7.1 fusion.2
  354.8 2.6 copy.150
  357.6 3.3 convolution_convert_fusion.9
  360.9 2.4 reshape.195
  363.3 3.7 fusion.60
  367.0 2.5 copy.123
  369.5 2.4 stack.23
  371.9 2.7 multiply_reduce_fusion.3
  377.3 2.6 copy.116
  379.9 2.4 stack.21
  382.3 2.4 fusion.63
  391.8 3.8 bitcast_convert_fusion.1
  396.5 2.9 fusion.101
  399.5 4.8 fusion.103
  404.6 4.7 fusion.102
  409.4 4.7 fusion.50
  414.1 7.4 bitcast_convert_fusion
  425.1 40.9 %reduce-scatter.25.cloned.1.call-done = f32[96,192]{1,0:T(8,128)} async-done(((f32[768,192]{1,0:T(8,128)}), f32[96,192]{1,0:T(8,128)}) %reduce-scatter.25.cloned.1.call-update) | async-done | bytes 73744
  467.6 65.5 %reduce-scatter.27.cloned.1.call-done = f32[96,384]{1,0:T(8,128)} async-done(((f32[768,384]{1,0:T(8,128)}), f32[96,384]{1,0:T(8,128)}) %reduce-scatter.27.cloned.1.call-update) | async-done | bytes 147472
  535.0 68.7 %all-reduce.16.cloned.1.call-done = (bf16[1024,768]{1,0:T(8,128)(2,1)}, bf16[1024,768]{1,0:T(8,128)(2,1)}) async-done(((bf16[1024,768]{1,0:T(8,128)(2,1)}, bf16[1024,768]{1,0:T(8,128)(2,1)}), (bf16[1024,768]{1,0:T(8,128)(2,1)}, bf16[1024,768]{1,0:T(8,128)(2,1)})) %all-reduce.16.cloned.1.call-update) | async-done | bytes 3145744 | tf_op jit(solution)/shard_map/psum | solution.py:26
  603.6 2.9 fusion.31
  606.6 38.2 %all-reduce = (f32[768]{0:T(1024)}, f32[768]{0:T(1024)}, f32[768]{0:T(1024)}, f32[768]{0:T(1024)}, f32[768]{0:T(1024)}, /*index=5*/f32[768]{0:T(1024)}, f32[768]...) all-reduce(f32[768]{0:T(1024)S(1)} %get-tuple-element.84, ...), channel_id=1, replica_groups=mesh['dp'=8,'tensor'=4] {'dp'}, use_global_device_ids=true, to_apply=%region_26.27 | all-reduce | flops 7680 | bytes 61440 | tf_op jit(solution)/shard_map/psum | solution.py:270
  644.8 4.1 add_convert_fusion.1
  648.9 2.2 fusion.18
  651.1 19.6 %reduce-scatter.19.cloned.1.call-done = f32[96,192]{1,0:T(8,128)} async-done(((f32[768,192]{1,0:T(8,128)}), f32[96,192]{1,0:T(8,128)}) %reduce-scatter.19.cloned.1.call-update) | async-done | bytes 73744 | tf_op jit(solution)/shard_map/reduce_scatter | solution.py:253
  670.7 73.0 %reduce-scatter.23.cloned.1.call-done = f32[768,96]{0,1:T(8,128)} async-done(((f32[768,768]{0,1:T(8,128)}), f32[768,96]{0,1:T(8,128)}) %reduce-scatter.23.cloned.1.call-update) | async-done | bytes 294928 | tf_op jit(solution)/shard_map/reduce_scatter | solution.py:257
  743.7 72.7 %reduce-scatter.21.cloned.1.call-done = f32[96,768]{1,0:T(8,128)} async-done(((f32[768,768]{1,0:T(8,128)}), f32[96,768]{1,0:T(8,128)}) %reduce-scatter.21.cloned.1.call-update) | async-done | bytes 294928 | tf_op jit(solution)/shard_map/reduce_scatter | solution.py:256
  816.4 73.0 %reduce-scatter.17.cloned.1.call-done = f32[96,3,192]{2,0,1:T(8,128)} async-done(((f32[768,3,192]{2,0,1:T(8,128)}), f32[96,3,192]{2,0,1:T(8,128)}) %reduce-scatter.17.cloned.1.call-update) | async-done | bytes 221200 | tf_op jit(solution)/shard_map/reduce_scatter | solution.py:251
  889.3 60.2 %reduce-scatter.15.cloned.1.call-done = bf16[16,256,192]{1,2,0:T(8,128)(2,1)} async-done(((bf16[16,256,768]{1,2,0:T(8,128)(2,1)}), bf16[16,256,192]{1,2,0:T(8,128)(2,1)}) %reduce-scatter.15.cloned.1.call-update) | async-done | bytes 1572880 | tf_op jit(solution)/shard_map/reduce_scatter | solution.py:198
  (224 shorter events, 62.8 us)
Async XLA Ops:
  7.2 197.1 %copy-start = (bf16[768,768]{1,0:T(8,128)(2,1)S(1)}, bf16[768,768]{1,0:T(8,128)(2,1)}, u32[]{:S(2)}) copy-start(bf16[768,768]{1,0:T(8,128)(2,1)} %param.39) | copy-start | bytes 3538948
  7.2 4.1 copy-start.1
  7.2 4.1 copy-start.45
  7.2 4.1 copy-start.60
  7.2 81.6 %all-reduce.8.cloned.1.call-start = ((), (), s32[]{:S(2)}) async-start(), calls=%async_computation.8 | async-start | bytes 3145728 | tf_op jit(solution)/shard_map/psum | solution.py:26
  11.3 2.3 copy-start.39
  37.8 6.3 copy-start.67
  37.8 51.0 %copy-start.36 = (f32[768]{0:T(1024)S(1)}, f32[768]{0:T(1024)}, u32[]{:S(2)}) copy-start(f32[768]{0:T(1024)} %param.28) | copy-start | bytes 9220
  43.1 93.8 %all-gather.2.cloned.1.call-start = ((), (), s32[]{:S(2)}) async-start(), calls=%async_computation.9 | async-start | bytes 7864320 | tf_op jit(solution)/shard_map/all_gather | solution.py:130
  43.8 153.9 %all-reduce.10.cloned.1.call-start = ((), (), s32[]{:S(2)}) async-start(), calls=%async_computation.10 | async-start | bytes 3145728 | tf_op jit(solution)/shard_map/psum | solution.py:26
  88.8 2.1 copy-start.4
  88.8 3.0 copy-start.49
  88.8 3.0 copy-start.65
  91.9 2.1 copy-start.35
  91.9 3.5 copy-start.41
  136.8 5.6 copy-start.14
  142.4 4.0 copy-start.33
  151.8 45.9 %copy-start.61 = (f32[768]{0:T(1024)S(1)}, f32[768]{0:T(1024)}, u32[]{:S(2)}) copy-start(f32[768]{0:T(1024)} %param.34) | copy-start | bytes 9220
  154.7 107.3 %all-reduce.12.cloned.1.call-start = ((), (), s32[]{:S(2)}) async-start(), calls=%async_computation.11 | async-start | bytes 3145728 | tf_op jit(solution)/shard_map/psum | solution.py:30
  204.9 10.3 %copy-start.25 = (f32[1024,768]{1,0:T(8,128)}, f32[1024,768]{1,0:T(8,128)S(1)}, u32[]{:S(2)}) copy-start(f32[1024,768]{1,0:T(8,128)S(1)} %fusion.100) | copy-start | bytes 9437188
  218.9 114.9 %all-reduce.14.cloned.1.call-start = ((), (), s32[]{:S(2)}) async-start(), calls=%async_computation.12 | async-start | bytes 3145728 | tf_op jit(solution)/shard_map/psum | solution.py:30
  262.0 4.4 copy-start.3
  262.0 4.4 copy-start.11
  262.0 4.4 copy-start.44
  262.0 4.4 copy-start.48
  266.4 4.8 copy-start.32
  275.1 4.1 copy-start.27
  275.1 4.1 copy-start.52
  279.2 2.2 copy-start.34
  290.7 132.7 %reduce-scatter.29.cloned.1.call-start = ((), (), s32[]{:S(2)}) async-start(), calls=%async_computation.20 | async-start | bytes 884736
  290.8 4.1 copy-start.15
  290.8 4.1 copy-start.21
  294.9 2.6 copy-start.9
  294.9 2.6 copy-start.23
  297.5 36.3 %copy-start.42 = (f32[1024]{0:T(1024)S(1)}, f32[1024]{0:T(1024)}, u32[]{:S(2)}) copy-start(f32[1024]{0:T(1024)} %copy-done.41) | copy-start | bytes 12292
  299.2 166.8 %reduce-scatter.25.cloned.1.call-start = ((), (), s32[]{:S(2)}) async-start(), calls=%async_computation.18 | async-start | bytes 884736
  333.8 4.2 copy-start.5
  333.8 4.2 copy-start.10
  333.8 4.2 copy-start.50
  338.0 5.1 copy-start.22
  344.8 188.3 %reduce-scatter.27.cloned.1.call-start = ((), (), s32[]{:S(2)}) async-start(), calls=%async_computation.19 | async-start | bytes 1327104
  344.8 2.9 copy-start.31
  347.7 7.1 copy-start.71
  357.5 246.1 %all-reduce.16.cloned.1.call-start = ((), (), s32[]{:S(2)}) async-start(), calls=%async_computation.21 | async-start | bytes 6291456 | tf_op jit(solution)/shard_map/psum | solution.py:26
  371.9 2.7 copy-start.18
  371.9 2.7 copy-start.37
  395.5 275.1 %reduce-scatter.19.cloned.1.call-start = ((), (), s32[]{:S(2)}) async-start(), calls=%async_computation.15 | async-start | bytes 884736 | tf_op jit(solution)/shard_map/reduce_scatter | solution.py:253
  399.4 344.2 %reduce-scatter.23.cloned.1.call-start = ((), (), s32[]{:S(2)}) async-start(), calls=%async_computation.17 | async-start | bytes 2654208 | tf_op jit(solution)/shard_map/reduce_scatter | solution.py:257
  404.3 412.1 %reduce-scatter.21.cloned.1.call-start = ((), (), s32[]{:S(2)}) async-start(), calls=%async_computation.16 | async-start | bytes 2654208 | tf_op jit(solution)/shard_map/reduce_scatter | solution.py:256
  409.3 4.8 copy-start.70
  409.3 480.0 %reduce-scatter.17.cloned.1.call-start = ((), (), s32[]{:S(2)}) async-start(), calls=%async_computation.14 | async-start | bytes 2654208 | tf_op jit(solution)/shard_map/reduce_scatter | solution.py:251
  414.1 535.5 %reduce-scatter.15.cloned.1.call-start = ((), (), s32[]{:S(2)}) async-start(), calls=%async_computation.13 | async-start | bytes 7864320 | tf_op jit(solution)/shard_map/reduce_scatter | solution.py:198
  421.5 182.1 %copy-start.40 = (f32[1024]{0:T(1024)S(1)}, f32[1024]{0:T(1024)}, u32[]{:S(2)}) copy-start(f32[1024]{0:T(1024)} %copy-done.39) | copy-start | bytes 12292
  421.5 182.1 %copy-start.46 = (f32[768]{0:T(1024)S(1)}, f32[768]{0:T(1024)}, u32[]{:S(2)}) copy-start(f32[768]{0:T(1024)} %param.24) | copy-start | bytes 9220
  421.6 185.0 %copy-start.53 = (f32[768]{0:T(1024)S(1)}, f32[768]{0:T(1024)}, u32[]{:S(2)}) copy-start(f32[768]{0:T(1024)} %get-tuple-element.107) | copy-start | bytes 9220
  421.6 185.0 %copy-start.54 = (f32[768]{0:T(1024)S(1)}, f32[768]{0:T(1024)}, u32[]{:S(2)}) copy-start(f32[768]{0:T(1024)} %get-tuple-element.80) | copy-start | bytes 9220
  421.6 185.0 %copy-start.55 = (f32[768]{0:T(1024)S(1)}, f32[768]{0:T(1024)}, u32[]{:S(2)}) copy-start(f32[768]{0:T(1024)} %get-tuple-element.90) | copy-start | bytes 9220
  421.6 185.0 %copy-start.56 = (f32[768]{0:T(1024)S(1)}, f32[768]{0:T(1024)}, u32[]{:S(2)}) copy-start(f32[768]{0:T(1024)} %get-tuple-element.109) | copy-start | bytes 9220
  421.6 185.0 %copy-start.57 = (f32[768]{0:T(1024)S(1)}, f32[768]{0:T(1024)}, u32[]{:S(2)}) copy-start(f32[768]{0:T(1024)} %get-tuple-element.82) | copy-start | bytes 9220
  421.6 185.0 %copy-start.58 = (f32[768]{0:T(1024)S(1)}, f32[768]{0:T(1024)}, u32[]{:S(2)}) copy-start(f32[768]{0:T(1024)} %get-tuple-element.89) | copy-start | bytes 9220
  421.6 185.0 %copy-start.63 = (f32[768]{0:T(1024)S(1)}, f32[768]{0:T(1024)}, u32[]{:S(2)}) copy-start(f32[768]{0:T(1024)} %get-tuple-element.104) | copy-start | bytes 9220
  421.6 223.2 %copy-start.66 = (f32[768]{0:T(1024)S(1)}, f32[768]{0:T(1024)}, u32[]{:S(2)}) copy-start(f32[768]{0:T(1024)} %param.40) | copy-start | bytes 9220
  644.8 4.1 copy-start.7
  644.8 4.1 copy-start.17
  (23 other events, 30.9 us)
Sparse Core Ops, SparseCore 0:
  43.2 45.5 all-reduce.7
  90.4 46.4 all-gather.1
  154.8 42.8 all-reduce.9
  219.1 42.8 all-reduce.11
  290.9 42.9 all-reduce.13
  337.0 63.3 reduce-scatter.28
  403.6 62.2 reduce-scatter.24
  469.4 63.7 reduce-scatter.26
  536.1 67.4 all-reduce.15
  607.4 63.2 reduce-scatter.18
  674.7 68.8 reduce-scatter.22
  747.6 68.7 reduce-scatter.20
  820.4 68.8 reduce-scatter.16
  892.3 57.2 reduce-scatter.14
where the time goes:
time: 964 us; the launch traced here: 956 us
  waiting for transfers between devices  659 us (68%)
  matrix products  105 us (11%)
  local copies, waits for them, and re-layouts  71.6 us (7%)
  other arithmetic  54.1 us (6%)
  blocking collectives  38.2 us (4%)
  between operations  15 us (2%)
  starting transfers between devices  13.1 us (1%)
    psum x3, waiting for transfers between devices, branch_total(): lax.psum(term_rows.astype(jnp.bfloat16), 'tensor').astype(jnp.float32)  153 us
    unnamed x17, waiting for transfers between devices  107 us
    reduce_scatter x1, waiting for transfers between devices, local(): lax.psum_scatter(grad_mlp_out_local, 'dp', scatter_dimension=1, tiled=True)  73 us
    reduce_scatter x1, waiting for transfers between devices, local(): lax.psum_scatter(grad_self_qkv_local, 'dp', scatter_dimension=0, tiled=True)  73 us
    reduce_scatter x1, waiting for transfers between devices, local(): lax.psum_scatter(grad_mlp_in_local, 'dp', scatter_dimension=0, tiled=True)  72.7 us
    psum x2, waiting for transfers between devices, input_total(): lax.psum(term_rows.astype(jnp.bfloat16), 'tensor').astype(jnp.float32)  61.2 us
    reduce_scatter x1, waiting for transfers between devices, local(): lax.psum_scatter(image_terms.astype(jnp.bfloat16), 'tensor', scatter_dime...  60.2 us
    all_gather x1, waiting for transfers between devices, local(): image_full = lax.all_gather(image_tokens, 'tensor', axis=2, tiled=True)  39 us
  transfers between devices with their start and end apart: 14, of which 13 were waited for; matrix products, arithmetic and copies ran while one was open for 13% of the time, Pallas kernels for 0%

commit v1 on v0

--- a/solution.py
+++ b/solution.py
@@ -23,7 +23,9 @@
 
 
 def branch_total(term_rows):
-    return lax.psum(term_rows.astype(jnp.bfloat16), "tensor").astype(jnp.float32)
+    return jnp.sum(lax.all_gather(term_rows.astype(jnp.bfloat16), "tensor"), axis=0).astype(
+        jnp.float32
+    )
 
 
 def input_total(term_rows):

time: 964 us -> 1010 us (1.048)
  other arithmetic: 54.1 us -> 80.8 us
  waiting for transfers between devices: 659 us -> 682 us
  starting transfers between devices: 13.1 us -> 2.19 us
    psum x3 -> x0, waiting for transfers between devices: 153 us -> none  [branch_total(): lax.psum(term_rows.astype(jnp.bfloat16), 'tensor').astype(jnp.float32)]
    all_gather x0 -> x3, waiting for transfers between devices: none -> 137 us  [branch_total(): lax.all_gather(term_rows.astype(jnp.bfloat16), 'tensor')]
    reduce_scatter x1, waiting for transfers between devices: 19.6 us -> 58.9 us  [local(): lax.psum_scatter(grad_cross_q_local, 'dp', scatter_dimension=0, tiled=True)]
    psum x2 -> x3, waiting for transfers between devices: 61.2 us -> 93 us  [input_total(): lax.psum(term_rows.astype(jnp.bfloat16), 'tensor').astype(jnp.float32)]
    unnamed x17 -> x18, waiting for transfers between devices: 107 us -> 88.4 us
    reduce_sum x0 -> x3, other arithmetic: none -> 15.4 us  [branch_total(): jnp.sum(lax.all_gather(term_rows.astype(jnp.bfloat16), 'tensor'), axis=0)]
    all_gather x1, waiting for transfers between devices: 39 us -> 27 us  [local(): image_full = lax.all_gather(image_tokens, 'tensor', axis=2, tiled=True)]
    unnamed x3, starting transfers between devices: 11.7 us -> 0.34 us
  transfers between devices with their start and end apart: 14 -> 15, of which waited for: 13 -> 14; matrix products, arithmetic and copies ran while one was open for 13% -> 14% of each run, Pallas kernels for 0% -> 0%
where the time goes in v1:
time: 1010 us; the launch traced here: 998 us
  waiting for transfers between devices  682 us (68%)
  matrix products  106 us (10%)
  other arithmetic  80.8 us (8%)
  local copies, waits for them, and re-layouts  72.5 us (7%)
  blocking collectives  38.1 us (4%)
  between operations  15.3 us (2%)
    all_gather x3, waiting for transfers between devices, branch_total(): lax.all_gather(term_rows.astype(jnp.bfloat16), 'tensor')  137 us
    psum x3, waiting for transfers between devices, input_total(): lax.psum(term_rows.astype(jnp.bfloat16), 'tensor').astype(jnp.float32)  93 us
    unnamed x18, waiting for transfers between devices  88.4 us
    reduce_scatter x1, waiting for transfers between devices, local(): lax.psum_scatter(grad_self_qkv_local, 'dp', scatter_dimension=0, tiled=True)  72.9 us
    reduce_scatter x1, waiting for transfers between devices, local(): lax.psum_scatter(grad_mlp_in_local, 'dp', scatter_dimension=0, tiled=True)  72.9 us
    reduce_scatter x1, waiting for transfers between devices, local(): lax.psum_scatter(grad_mlp_out_local, 'dp', scatter_dimension=1, tiled=True)  72.6 us
    reduce_scatter x1, waiting for transfers between devices, local(): lax.psum_scatter(image_terms.astype(jnp.bfloat16), 'tensor', scatter_dime...  60.2 us
    reduce_scatter x1, waiting for transfers between devices, local(): lax.psum_scatter(grad_cross_q_local, 'dp', scatter_dimension=0, tiled=True)  58.9 us
  transfers between devices with their start and end apart: 15, of which 14 were waited for; matrix products, arithmetic and copies ran while one was open for 14% of the time, Pallas kernels for 0%

profile of v1, /device:TPU:0, one launch (start us, length us, event | category | flops | bytes accessed | tf_op | source)
XLA Modules:
  0.0 997.7 jit_solution(14129401830106081236)
XLA Ops:
  14.8 4.2 reshape.302
  19.0 3.1 fusion.106
  24.0 2.7 copy.154
  31.6 3.6 fusion.67
  35.3 2.5 copy.103
  37.8 2.4 reshape.303
  40.3 2.8 convolution_convert_fusion.5
  44.8 47.6 %all-gather.10.cloned.1.call-done = bf16[4096,768]{1,0:T(8,128)(2,1)} async-done(((bf16[1024,768]{1,0:T(8,128)(2,1)}), bf16[4096,768]{1,0:T(8,128)(2,1)}) %all-gather.10.cloned.1.call-update) | async-done | bytes 6291472 | tf_op jit(solution)/shard_map/all_gather | solution.py:26
  92.4 5.3 reduce_sum.273
  97.7 3.6 fusion.100
  101.9 3.0 multiply_reduce_fusion.2
  113.3 27.0 %all-gather.8.cloned.1.call-done = bf16[16,256,768]{1,2,0:T(8,128)(2,1)} async-done(((bf16[16,256,192]{1,2,0:T(8,128)(2,1)}), bf16[16,256,768]{1,2,0:T(8,128)(2,1)}) %all-gather.8.cloned.1.call-update) | async-done | bytes 6291472 | tf_op jit(solution)/shard_map/all_gather | solution.py:132
  140.3 5.6 fusion.49
  146.6 3.2 fusion.108
  155.3 2.9 convolution_convert_fusion.4
  158.6 2.7 bitcast_convert_fusion.2
  161.2 43.5 %all-gather.12.cloned.1.call-done = bf16[4096,768]{1,0:T(8,128)(2,1)} async-done(((bf16[1024,768]{1,0:T(8,128)(2,1)}), bf16[4096,768]{1,0:T(8,128)(2,1)}) %all-gather.12.cloned.1.call-update) | async-done | bytes 6291472 | tf_op jit(solution)/shard_map/all_gather | solution.py:26
  204.8 5.4 reduce_sum.277
  210.1 4.1 add_convert_fusion
  218.8 3.0 subtract_multiply_fusion
  224.4 10.2 %convert_reduce_fusion.5 = (f32[768]{0:T(1024)}, bf16[1024,768]{1,0:T(8,128)(2,1)S(1)}, f32[1024,768]{1,0:T(8,128)}) fusion(f32[1024,768]{1,0:T(8,128)S(1)} %fusion.93, f32[768]{0:T(1024)S(1)} %copy-done.57, bf16[1024,768]{1,0:T(8,128)(2,1)S(1)} %copy-done.25, bf16[768,768]{1,0:T(8,128)(2,1)S(1)} %copy-done), kind=kOutput, calls=%fused_computation.64 | convolution fusion | flops 1266941184 | bytes 10622976 | tf_op jit(solution)/shard_map/rd,fd->rf/dot_general | solution.py:168
  235.9 2.6 convolution_convert_fusion.2
  239.0 42.5 %all-reduce.5.cloned.1.call-done = bf16[1024,768]{1,0:T(8,128)(2,1)} async-done(((bf16[1024,768]{1,0:T(8,128)(2,1)}), bf16[1024,768]{1,0:T(8,128)(2,1)}) %all-reduce.5.cloned.1.call-update) | async-done | bytes 1572880 | tf_op jit(solution)/shard_map/psum | solution.py:32
  281.5 4.1 fusion.29
  285.6 2.4 fusion.102
  293.6 4.0 multiply_reduce_fusion
  301.3 2.6 copy.110
  303.9 2.4 reshape.309
  306.3 2.8 convolution_convert_fusion.1
  309.3 3.7 convolution_bitcast_fusion
  313.2 39.1 %all-reduce.7.cloned.1.call-done = bf16[1024,768]{1,0:T(8,128)(2,1)} async-done(((bf16[1024,768]{1,0:T(8,128)(2,1)}), bf16[1024,768]{1,0:T(8,128)(2,1)}) %all-reduce.7.cloned.1.call-update) | async-done | bytes 1572880 | tf_op jit(solution)/shard_map/psum | solution.py:32
  352.3 4.4 fusion.30
  356.7 3.4 fusion.104
  365.6 3.7 fusion.68
  369.3 2.5 copy.123
  371.8 2.4 stack.23
  374.2 2.7 multiply_reduce_fusion.3
  379.6 2.6 copy.116
  394.1 3.8 bitcast_convert_fusion.1
  398.1 3.3 multiply_convert_fusion
  403.3 2.7 convolution_convert_fusion
  406.0 7.0 fusion.2
  413.0 2.7 copy.150
  415.8 3.3 multiply_convert_fusion.2
  420.2 2.5 convolution_convert_fusion.3
  422.9 3.0 fusion.110
  425.9 4.8 fusion.111
  430.8 5.3 fusion.92
  436.2 4.7 fusion.54
  441.2 7.4 bitcast_convert_fusion
  452.2 11.5 %all-reduce.9.cloned.1.call-done = bf16[1024,768]{1,0:T(8,128)(2,1)} async-done(((bf16[1024,768]{1,0:T(8,128)(2,1)}), bf16[1024,768]{1,0:T(8,128)(2,1)}) %all-reduce.9.cloned.1.call-update) | async-done | bytes 1572880 | tf_op jit(solution)/shard_map/psum | solution.py:32
  463.7 2.9 fusion.31
  466.7 38.1 %all-reduce = (f32[768]{0:T(1024)}, f32[768]{0:T(1024)}, f32[768]{0:T(1024)}, f32[768]{0:T(1024)}, f32[768]{0:T(1024)}, /*index=5*/f32[768]{0:T(1024)}, f32[768]...) all-reduce(f32[768]{0:T(1024)S(1)} %get-tuple-element.84, ...), channel_id=1, replica_groups=mesh['dp'=8,'tensor'=4] {'dp'}, use_global_device_ids=true, to_apply=%region_26.27 | all-reduce | flops 7680 | bytes 61440 | tf_op jit(solution)/shard_map/psum | solution.py:272
  504.8 3.8 fusion.18
  508.6 21.8 %reduce-scatter.25.cloned.1.call-done = f32[96,192]{1,0:T(8,128)} async-done(((f32[768,192]{1,0:T(8,128)}), f32[96,192]{1,0:T(8,128)}) %reduce-scatter.25.cloned.1.call-update) | async-done | bytes 73744
  532.0 65.7 %reduce-scatter.27.cloned.1.call-done = f32[96,384]{1,0:T(8,128)} async-done(((f32[768,384]{1,0:T(8,128)}), f32[96,384]{1,0:T(8,128)}) %reduce-scatter.27.cloned.1.call-update) | async-done | bytes 147472
  599.6 45.5 %all-gather.14.cloned.1.call-done = bf16[4096,768]{1,0:T(8,128)(2,1)} async-done(((bf16[1024,768]{1,0:T(8,128)(2,1)}), bf16[4096,768]{1,0:T(8,128)(2,1)}) %all-gather.14.cloned.1.call-update) | async-done | bytes 6291472 | tf_op jit(solution)/shard_map/all_gather | solution.py:26
  645.1 4.7 reduce_sum.280
  649.9 3.5 fusion.33
  653.4 58.9 %reduce-scatter.19.cloned.1.call-done = f32[96,192]{1,0:T(8,128)} async-done(((f32[768,192]{1,0:T(8,128)}), f32[96,192]{1,0:T(8,128)}) %reduce-scatter.19.cloned.1.call-update) | async-done | bytes 73744 | tf_op jit(solution)/shard_map/reduce_scatter | solution.py:255
  712.2 72.6 %reduce-scatter.23.cloned.1.call-done = f32[768,96]{0,1:T(8,128)} async-done(((f32[768,768]{0,1:T(8,128)}), f32[768,96]{0,1:T(8,128)}) %reduce-scatter.23.cloned.1.call-update) | async-done | bytes 294928 | tf_op jit(solution)/shard_map/reduce_scatter | solution.py:259
  784.8 72.9 %reduce-scatter.21.cloned.1.call-done = f32[96,768]{1,0:T(8,128)} async-done(((f32[768,768]{1,0:T(8,128)}), f32[96,768]{1,0:T(8,128)}) %reduce-scatter.21.cloned.1.call-update) | async-done | bytes 294928 | tf_op jit(solution)/shard_map/reduce_scatter | solution.py:258
  857.7 72.9 %reduce-scatter.17.cloned.1.call-done = f32[96,3,192]{2,0,1:T(8,128)} async-done(((f32[768,3,192]{2,0,1:T(8,128)}), f32[96,3,192]{2,0,1:T(8,128)}) %reduce-scatter.17.cloned.1.call-update) | async-done | bytes 221200 | tf_op jit(solution)/shard_map/reduce_scatter | solution.py:253
  930.6 60.2 %reduce-scatter.15.cloned.1.call-done = bf16[16,256,192]{1,2,0:T(8,128)(2,1)} async-done(((bf16[16,256,768]{1,2,0:T(8,128)(2,1)}), bf16[16,256,192]{1,2,0:T(8,128)(2,1)}) %reduce-scatter.15.cloned.1.call-update) | async-done | bytes 1572880 | tf_op jit(solution)/shard_map/reduce_scatter | solution.py:200
  (233 shorter events, 80.6 us)
Async XLA Ops:
  7.2 216.4 %copy-start = (bf16[768,768]{1,0:T(8,128)(2,1)S(1)}, bf16[768,768]{1,0:T(8,128)(2,1)}, u32[]{:S(2)}) copy-start(bf16[768,768]{1,0:T(8,128)(2,1)} %param.39) | copy-start | bytes 3538948
  7.2 4.1 copy-start.1
  7.2 4.1 copy-start.40
  7.2 4.1 copy-start.59
  7.2 85.1 %all-gather.10.cloned.1.call-start = ((), (), s32[]{:S(2)}) async-start(), calls=%async_computation.17 | async-start | bytes 7864320 | tf_op jit(solution)/shard_map/all_gather | solution.py:26
  9.2 4.4 copy-start.35
  37.8 6.3 copy-start.64
  43.1 97.2 %all-gather.8.cloned.1.call-start = ((), (), s32[]{:S(2)}) async-start(), calls=%async_computation.8 | async-start | bytes 7864320 | tf_op jit(solution)/shard_map/all_gather | solution.py:132
  43.9 160.9 %all-gather.12.cloned.1.call-start = ((), (), s32[]{:S(2)}) async-start(), calls=%async_computation.18 | async-start | bytes 7864320 | tf_op jit(solution)/shard_map/all_gather | solution.py:26
  92.4 5.3 copy-start.39
  105.6 3.6 copy-start.32
  105.6 3.6 copy-start.42
  105.6 3.6 copy-start.44
  105.6 3.6 copy-start.46
  105.6 3.6 copy-start.60
  140.3 5.6 copy-start.12
  145.9 4.0 copy-start.30
  158.2 123.2 %all-reduce.5.cloned.1.call-start = ((), (), s32[]{:S(2)}) async-start(), calls=%async_computation.9 | async-start | bytes 3145728 | tf_op jit(solution)/shard_map/psum | solution.py:32
  218.8 3.0 copy-start.51
  218.8 3.0 copy-start.65
  218.8 3.0 copy-start.68
  224.4 10.2 %copy-start.20 = (f32[1024,768]{1,0:T(8,128)}, f32[1024,768]{1,0:T(8,128)S(1)}, u32[]{:S(2)}) copy-start(f32[1024,768]{1,0:T(8,128)S(1)} %fusion.93) | copy-start | bytes 9437188
  238.4 113.8 %all-reduce.7.cloned.1.call-start = ((), (), s32[]{:S(2)}) async-start(), calls=%async_computation.10 | async-start | bytes 3145728 | tf_op jit(solution)/shard_map/psum | solution.py:32
  281.4 4.1 copy-start.8
  281.5 4.1 copy-start.9
  285.6 4.2 copy-start.27
  293.6 4.1 copy-start.22
  293.6 4.1 copy-start.49
  309.2 43.1 %copy-start.43 = (f32[768]{0:T(1024)S(1)}, f32[768]{0:T(1024)}, u32[]{:S(2)}) copy-start(f32[768]{0:T(1024)} %param.29) | copy-start | bytes 9220
  309.2 43.1 %copy-start.45 = (f32[1024]{0:T(1024)S(1)}, f32[1024]{0:T(1024)}, u32[]{:S(2)}) copy-start(f32[1024]{0:T(1024)} %div.64) | copy-start | bytes 12292
  309.2 43.1 %copy-start.47 = (f32[1024]{0:T(1024)S(1)}, f32[1024]{0:T(1024)}, u32[]{:S(2)}) copy-start(f32[1024]{0:T(1024)} %rsqrt.37) | copy-start | bytes 12292
  309.2 141.4 %reduce-scatter.29.cloned.1.call-start = ((), (), s32[]{:S(2)}) async-start(), calls=%async_computation.22 | async-start | bytes 884736
  313.0 150.7 %all-reduce.9.cloned.1.call-start = ((), (), s32[]{:S(2)}) async-start(), calls=%async_computation.11 | async-start | bytes 3145728 | tf_op jit(solution)/shard_map/psum | solution.py:32
  352.3 4.4 copy-start.5
  352.3 4.4 copy-start.15
  356.7 5.1 copy-start.28
  374.2 2.7 copy-start.16
  374.2 2.7 copy-start.33
  394.1 3.9 copy-start.13
  398.0 132.4 %reduce-scatter.25.cloned.1.call-start = ((), (), s32[]{:S(2)}) async-start(), calls=%async_computation.20 | async-start | bytes 884736
  398.0 3.3 copy-start.3
  398.1 3.3 copy-start.18
  403.0 194.7 %reduce-scatter.27.cloned.1.call-start = ((), (), s32[]{:S(2)}) async-start(), calls=%async_computation.21 | async-start | bytes 1327104
  406.0 7.0 copy-start.70
  413.0 2.7 copy-start.58
  415.7 229.4 %all-gather.14.cloned.1.call-start = ((), (), s32[]{:S(2)}) async-start(), calls=%async_computation.19 | async-start | bytes 7864320 | tf_op jit(solution)/shard_map/all_gather | solution.py:26
  422.8 289.4 %reduce-scatter.19.cloned.1.call-start = ((), (), s32[]{:S(2)}) async-start(), calls=%async_computation.14 | async-start | bytes 884736 | tf_op jit(solution)/shard_map/reduce_scatter | solution.py:255
  425.8 4.9 copy-start.52
  425.8 4.9 copy-start.69
  425.9 359.0 %reduce-scatter.23.cloned.1.call-start = ((), (), s32[]{:S(2)}) async-start(), calls=%async_computation.16 | async-start | bytes 2654208 | tf_op jit(solution)/shard_map/reduce_scatter | solution.py:259
  430.7 427.0 %reduce-scatter.21.cloned.1.call-start = ((), (), s32[]{:S(2)}) async-start(), calls=%async_computation.15 | async-start | bytes 2654208 | tf_op jit(solution)/shard_map/reduce_scatter | solution.py:258
  436.1 5.1 copy-start.67
  436.1 494.5 %reduce-scatter.17.cloned.1.call-start = ((), (), s32[]{:S(2)}) async-start(), calls=%async_computation.13 | async-start | bytes 2654208 | tf_op jit(solution)/shard_map/reduce_scatter | solution.py:253
  440.9 549.9 %reduce-scatter.15.cloned.1.call-start = ((), (), s32[]{:S(2)}) async-start(), calls=%async_computation.12 | async-start | bytes 7864320 | tf_op jit(solution)/shard_map/reduce_scatter | solution.py:200
  448.7 15.1 %copy-start.36 = (f32[1024]{0:T(1024)S(1)}, f32[1024]{0:T(1024)}, u32[]{:S(2)}) copy-start(f32[1024]{0:T(1024)} %copy-done.35) | copy-start | bytes 12292
  448.7 15.1 %copy-start.38 = (f32[1024]{0:T(1024)S(1)}, f32[1024]{0:T(1024)}, u32[]{:S(2)}) copy-start(f32[1024]{0:T(1024)} %copy-done.37) | copy-start | bytes 12292
  448.7 15.1 %copy-start.41 = (f32[768]{0:T(1024)S(1)}, f32[768]{0:T(1024)}, u32[]{:S(2)}) copy-start(f32[768]{0:T(1024)} %param.24) | copy-start | bytes 9220
  448.7 17.9 %copy-start.50 = (f32[768]{0:T(1024)S(1)}, f32[768]{0:T(1024)}, u32[]{:S(2)}) copy-start(f32[768]{0:T(1024)} %get-tuple-element.107) | copy-start | bytes 9220
  448.7 17.9 %copy-start.53 = (f32[768]{0:T(1024)S(1)}, f32[768]{0:T(1024)}, u32[]{:S(2)}) copy-start(f32[768]{0:T(1024)} %get-tuple-element.82) | copy-start | bytes 9220
  448.7 17.9 %copy-start.54 = (f32[768]{0:T(1024)S(1)}, f32[768]{0:T(1024)}, u32[]{:S(2)}) copy-start(f32[768]{0:T(1024)} %get-tuple-element.89) | copy-start | bytes 9220
  448.7 17.9 %copy-start.55 = (f32[768]{0:T(1024)S(1)}, f32[768]{0:T(1024)}, u32[]{:S(2)}) copy-start(f32[768]{0:T(1024)} %get-tuple-element.80) | copy-start | bytes 9220
  448.7 17.9 %copy-start.56 = (f32[768]{0:T(1024)S(1)}, f32[768]{0:T(1024)}, u32[]{:S(2)}) copy-start(f32[768]{0:T(1024)} %get-tuple-element.90) | copy-start | bytes 9220
  448.7 17.9 %copy-start.61 = (f32[768]{0:T(1024)S(1)}, f32[768]{0:T(1024)}, u32[]{:S(2)}) copy-start(f32[768]{0:T(1024)} %get-tuple-element.102) | copy-start | bytes 9220
  645.1 4.7 copy-start.63
  (23 other events, 38.4 us)
Sparse Core Ops, SparseCore 0:
  43.2 49.0 all-gather.9
  93.9 46.3 all-gather.7
  158.4 46.3 all-gather.11
  238.6 42.8 all-reduce.4
  309.3 42.8 all-reduce.6
  355.4 63.3 reduce-scatter.28
  421.7 41.9 all-reduce.8
  467.0 63.3 reduce-scatter.24
  533.8 63.8 reduce-scatter.26
  599.7 45.3 all-gather.13
  649.0 63.1 reduce-scatter.18
  716.2 68.6 reduce-scatter.22
  788.9 68.7 reduce-scatter.20
  861.6 68.9 reduce-scatter.16
  933.5 57.1 reduce-scatter.14
